TPU v7x, 32 devices: a whole 2x2x4 slice. The times are simulated.
32 devices in a mesh: slab: 8 (over z, y), col: 4 (over x, core).
Axes of the slice: x: 2, y: 2, z: 4, core: 2. Of those that a mesh axis runs over, the one named last changes fastest.
Arguments:
- classes: int32 [64, 512], P(('slab', 'col')), may hold values from 0 to 15
- across_coeff: float32 [16], replicated, may hold values from 0.5 to 5
- along_coeff: float32 [16], replicated, may hold values from 0.05 to 0.5
Outputs:
- piece_maps: float32 [32768, 1024], P(('slab', 'col'))
- root_map: float32 [1024, 1024], P(('slab', 'col'))
All inputs are finite; a program needn't handle non-finite values.
Results may differ from a plain program's by a relative error of at most 0.0003.
Values sent between devices are 32-bit elements; how exact they have to be, the bound alone decides.
A program may use at most 128 MiB of HBM per device.

v0:
```python
import jax
import jax.numpy as jnp
from jax import lax
from jax.sharding import PartitionSpec as P


def swapped(block, axis, stride):
    count = lax.axis_size(axis)
    route = []
    for low in range(count):
        high = low | 1 << stride
        if high != low and high < count:
            route += [(low, high), (high, low)]
    return lax.ppermute(block, axis, route)


def lookup(classes, values_table):
    levels = jnp.arange(values_table.shape[0], dtype=jnp.int32)
    matches = classes[:, None, :] == levels[None, :, None]
    return jnp.sum(jnp.where(matches, values_table[None, :, None], 0.0), axis=1)


def strip_map(along_col, across_col):
    half_size = along_col.shape[0]
    row_index = lax.broadcasted_iota(jnp.int32, (half_size, half_size), 0)
    col_index = lax.broadcasted_iota(jnp.int32, (half_size, half_size), 1)
    shifted = jnp.roll(along_col, 1)
    vertical = jnp.where(row_index == col_index, (along_col + shifted)[None, :], 0.0)
    vertical = vertical - jnp.where(
        col_index == (row_index + 1) % half_size, along_col[:, None], 0.0
    )
    vertical = vertical - jnp.where(
        row_index == (col_index + 1) % half_size, along_col[None, :], 0.0
    )
    across_diag = jnp.where(row_index == col_index, across_col[None, :], 0.0)
    upper_rows = jnp.concatenate([vertical + across_diag, -across_diag], axis=1)
    lower_rows = jnp.concatenate([-across_diag, across_diag], axis=1)
    return jnp.concatenate([upper_rows, lower_rows], axis=0)


def quarters(full_map):
    half_size = full_map.shape[0] // 2
    return (
        full_map[:half_size, :half_size],
        full_map[:half_size, half_size:],
        full_map[half_size:, :half_size],
        full_map[half_size:, half_size:],
    )


def blocked_factor(matrix):
    size_total = matrix.shape[0]
    panel = 128
    columns = []
    remaining = matrix
    for start in range(0, size_total, panel):
        head = remaining[:panel, :panel]
        head_factor = jnp.linalg.cholesky(head)
        if remaining.shape[0] > panel:
            below = remaining[panel:, :panel]
            below_factor = lax.linalg.triangular_solve(
                head_factor, below, left_side=False, lower=True, transpose_a=True
            )
            remaining = remaining[panel:, panel:] - lax.dot_general(
                below_factor,
                below_factor,
                (((1,), (1,)), ((), ())),
                precision=lax.Precision.HIGHEST,
            )
            block_column = jnp.concatenate([head_factor, below_factor], axis=0)
        else:
            block_column = head_factor
        if start > 0:
            block_column = jnp.concatenate(
                [jnp.zeros((start, panel), matrix.dtype), block_column], axis=0
            )
        columns.append(block_column)
    return jnp.concatenate(columns, axis=1)


def merge_blocks(
    left_upper, left_lower_left, left_lower, right_upper, right_upper_right, right_lower
):
    half_size = left_upper.shape[0]
    factor = blocked_factor(left_lower + right_upper)
    coupled = jnp.concatenate([left_lower_left, right_upper_right], axis=1)
    scaled = lax.linalg.triangular_solve(factor, coupled, left_side=True, lower=True)
    product = lax.dot_general(
        scaled, scaled, (((0,), (0,)), ((), ())), precision=lax.Precision.HIGHEST
    )
    zero_block = jnp.zeros((half_size, half_size), left_upper.dtype)
    diagonal_part = jnp.concatenate(
        [
            jnp.concatenate([left_upper, zero_block], axis=1),
            jnp.concatenate([zero_block, right_lower], axis=1),
        ],
        axis=0,
    )
    return diagonal_part - product


def merge_maps(left_map, right_map):
    left_upper, left_upper_right, left_lower_left, left_lower = quarters(left_map)
    right_upper, right_upper_right, right_lower_left, right_lower = quarters(right_map)
    return merge_blocks(
        left_upper, left_lower_left, left_lower, right_upper, right_upper_right, right_lower
    )


def level_payload(merged, is_right):
    upper, upper_right, lower_left, lower = quarters(merged)
    middle = jnp.where(is_right, upper_right, lower_left)
    payload = jnp.stack([upper, middle, lower])
    return payload


def joined(merged, received, is_right):
    upper, upper_right, lower_left, lower = quarters(merged)
    partner_upper = received[0]
    partner_middle = received[1]
    partner_lower = received[2]
    left_upper = jnp.where(is_right, partner_upper, upper)
    left_lower_left = jnp.where(is_right, partner_middle, lower_left)
    left_lower = jnp.where(is_right, partner_lower, lower)
    right_upper = jnp.where(is_right, upper, partner_upper)
    right_upper_right = jnp.where(is_right, upper_right, partner_middle)
    right_lower = jnp.where(is_right, lower, partner_lower)
    return merge_blocks(
        left_upper, left_lower_left, left_lower, right_upper, right_upper_right, right_lower
    )


def local(classes, across_coeff, along_coeff):
    across = lookup(classes, across_coeff)
    along = lookup(classes, along_coeff)
    own_map = strip_map(along[0], across[0])
    own_map = merge_maps(own_map, strip_map(along[1], across[1]))
    col_levels = lax.axis_size("col").bit_length() - 1
    slab_levels = lax.axis_size("slab").bit_length() - 1
    merged = own_map
    for height in range(col_levels):
        is_right = lax.axis_index("col") >> height & 1 == 1
        received = swapped(level_payload(merged, is_right), "col", height)
        merged = joined(merged, received, is_right)
    for height in range(slab_levels):
        is_right = lax.axis_index("slab") >> height & 1 == 1
        received = swapped(level_payload(merged, is_right), "slab", height)
        merged = joined(merged, received, is_right)
    share_rows = merged.shape[0] // lax.axis_size(("slab", "col"))
    root_rows = lax.dynamic_slice_in_dim(
        merged, lax.axis_index(("slab", "col")) * share_rows, share_rows, 0
    )
    return (own_map, root_rows)


def solution(mesh):
    placed = (P(("slab", "col"), None), P(), P())
    return jax.shard_map(
        local,
        mesh=mesh,
        in_specs=placed,
        out_specs=(P(("slab", "col"), None), P(("slab", "col"), None)),
        check_vma=False,
    )
```

profile of v0, /device:TPU:0, one launch (start us, length us, event | category | flops | bytes accessed | tf_op | source)
XLA Modules:
  0.0 1403.1 jit_solution(8966008555084529291)
XLA Ops:
  5.5 11.7 cholesky.374
  31.4 11.7 cholesky.385
  44.4 10.0 custom-call.35
  57.2 11.7 cholesky.396
  80.8 11.7 cholesky.407
  93.9 11.2 fusion.91
  105.1 11.4 while.12
  116.5 39.3 %custom-call.37 = f32[4,128,128]{1,2,0:T(8,128)S(1)} custom-call(f32[4,128,128]{2,1,0:T(8,128)S(1)} %get-tuple-element.45), custom_call_target="InvertDiagBlocksLowerTriangular" | custom-call | tf_op jit(solution)/shard_map/triangular_solve/custom-call.4 | solution.py:87
  194.9 11.7 cholesky.418
  208.0 9.8 custom-call.38
  222.7 11.9 cholesky.429
  248.5 11.7 cholesky.440
  272.1 12.1 cholesky.451
  286.6 11.7 while.13
  298.3 39.3 %custom-call.41 = f32[4,128,128]{1,2,0:T(8,128)S(1)} custom-call(f32[4,128,128]{2,1,0:T(8,128)S(1)} %get-tuple-element.46), custom_call_target="InvertDiagBlocksLowerTriangular" | custom-call | tf_op jit(solution)/shard_map/triangular_solve/custom-call.4 | solution.py:87
  364.7 68.7 %collective-permute-done.1 = f32[3,512,512]{1,2,0:T(8,128)} collective-permute-done((f32[3,512,512]{1,2,0:T(8,128)}, f32[3,512,512]{1,2,0:T(8,128)}, u32[]{:S(2)}, u32[]{:S(2)}) %collective-permute-start.1) | collective-permute-done | bytes 3145760 | tf_op jit(solution)/shard_map/ppermute | solution.py:14
  441.0 11.7 cholesky.462
  468.9 11.9 cholesky.473
  494.7 11.7 cholesky.484
  507.8 10.2 custom-call.44
  518.7 11.7 cholesky.495
  532.8 11.9 while.14
  544.7 39.5 %custom-call.45 = f32[4,128,128]{1,2,0:T(8,128)S(1)} custom-call(f32[4,128,128]{2,1,0:T(8,128)S(1)} %get-tuple-element.47), custom_call_target="InvertDiagBlocksLowerTriangular" | custom-call | tf_op jit(solution)/shard_map/triangular_solve/custom-call.4 | solution.py:87
  610.2 68.1 %collective-permute-done.2 = f32[3,512,512]{1,2,0:T(8,128)} collective-permute-done((f32[3,512,512]{1,2,0:T(8,128)}, f32[3,512,512]{1,2,0:T(8,128)}, u32[]{:S(2)}, u32[]{:S(2)}) %collective-permute-start.2) | collective-permute-done | bytes 3145760 | tf_op jit(solution)/shard_map/ppermute | solution.py:14
  685.9 11.7 cholesky.506
  713.8 12.1 cholesky.517
  739.8 11.7 cholesky.528
  752.9 10.0 custom-call.48
  763.5 11.7 cholesky.539
  777.7 11.9 while.15
  789.6 39.5 %custom-call.49 = f32[4,128,128]{1,2,0:T(8,128)S(1)} custom-call(f32[4,128,128]{2,1,0:T(8,128)S(1)} %get-tuple-element.48), custom_call_target="InvertDiagBlocksLowerTriangular" | custom-call | tf_op jit(solution)/shard_map/triangular_solve/custom-call.4 | solution.py:87
  855.1 67.5 %collective-permute-done.3 = f32[3,512,512]{1,2,0:T(8,128)} collective-permute-done((f32[3,512,512]{1,2,0:T(8,128)}, f32[3,512,512]{1,2,0:T(8,128)}, u32[]{:S(2)}, u32[]{:S(2)}) %collective-permute-start.3) | collective-permute-done | bytes 3145760 | tf_op jit(solution)/shard_map/ppermute | solution.py:14
  930.2 11.7 cholesky.550
  958.0 11.9 cholesky.561
  983.9 11.7 cholesky.572
  996.9 10.0 custom-call.52
  1007.6 11.7 cholesky.583
  1021.8 11.9 while.16
  1033.6 39.7 %custom-call.53 = f32[4,128,128]{1,2,0:T(8,128)S(1)} custom-call(f32[4,128,128]{2,1,0:T(8,128)S(1)} %get-tuple-element.49), custom_call_target="InvertDiagBlocksLowerTriangular" | custom-call | tf_op jit(solution)/shard_map/triangular_solve/custom-call.4 | solution.py:87
  1105.2 128.9 %collective-permute-done.4 = f32[3,512,512]{1,2,0:T(8,128)} collective-permute-done((f32[3,512,512]{1,2,0:T(8,128)}, f32[3,512,512]{1,2,0:T(8,128)}, u32[]{:S(2)}, u32[]{:S(2)}) %collective-permute-start.4) | collective-permute-done | bytes 3145760 | tf_op jit(solution)/shard_map/ppermute | solution.py:14
  1241.6 11.7 cholesky.594
  1254.6 9.8 custom-call.54
  1269.3 11.7 cholesky.605
  1282.5 10.2 custom-call.55
  1295.4 11.7 cholesky.616
  1319.0 11.9 cholesky.627
  1333.2 11.1 while.17
  1344.3 39.3 %custom-call.57 = f32[4,128,128]{1,2,0:T(8,128)S(1)} custom-call(f32[4,128,128]{2,1,0:T(8,128)S(1)} %get-tuple-element.50), custom_call_target="InvertDiagBlocksLowerTriangular" | custom-call | tf_op jit(solution)/shard_map/triangular_solve/custom-call.4 | solution.py:87
  (425 shorter events, 466.3 us)
Async XLA Ops:
  29.6 0.8 copy-start.12
  155.9 0.7 copy-start.27
  159.9 2.8 copy-start.28
  163.3 3.9 copy-start.18
  177.3 1.9 copy-start
  181.2 6.1 collective-permute-start
  192.9 1.0 copy-start.11
  220.9 0.8 copy-start.13
  337.6 0.7 copy-start.29
  340.2 4.3 copy-start.30
  348.8 1.2 copy-start.25
  348.8 1.5 copy-start.26
  357.8 2.0 copy-start.2
  361.9 71.6 %collective-permute-start.1 = (f32[3,512,512]{1,2,0:T(8,128)}, f32[3,512,512]{1,2,0:T(8,128)}, u32[]{:S(2)}, u32[]{:S(2)}) collective-permute-start(f32[3,512,512]{1,2,0:T(8,128)} %pad_maximum_fusion.13), channel_id=1, source_target_pairs={{0,2},{2,0},{1,3},{3,1},{4,6},{6,4},{5,7},{7,5},{8,10},{10,8},{9,1... | collective-permute-start | bytes 9437192 | tf_op jit(solution)/shard_map/ppermute | solution.py:14
  439.1 1.0 copy-start.7
  467.1 0.8 copy-start.14
  584.2 0.7 copy-start.31
  586.7 4.3 copy-start.32
  595.4 1.2 copy-start.19
  595.4 1.5 copy-start.20
  604.4 2.0 copy-start.4
  608.5 69.9 %collective-permute-start.2 = (f32[3,512,512]{1,2,0:T(8,128)}, f32[3,512,512]{1,2,0:T(8,128)}, u32[]{:S(2)}, u32[]{:S(2)}) collective-permute-start(f32[3,512,512]{1,2,0:T(8,128)} %pad_maximum_fusion.14), channel_id=1, source_target_pairs={{0,4},{4,0},{8,12},{12,8},{16,20},{20,16},{24,28},{28,24},{1,5},{5... | collective-permute-start | bytes 9437192 | tf_op jit(solution)/shard_map/ppermute | solution.py:14
  684.0 1.0 copy-start.8
  712.0 0.8 copy-start.15
  829.1 0.7 copy-start.33
  831.6 4.3 copy-start.34
  840.3 1.2 copy-start.21
  840.3 1.5 copy-start.22
  849.5 2.0 copy-start.3
  853.6 69.0 %collective-permute-start.3 = (f32[3,512,512]{1,2,0:T(8,128)}, f32[3,512,512]{1,2,0:T(8,128)}, u32[]{:S(2)}, u32[]{:S(2)}) collective-permute-start(f32[3,512,512]{1,2,0:T(8,128)} %pad_maximum_fusion.15), channel_id=1, source_target_pairs={{0,8},{8,0},{4,12},{12,4},{16,24},{24,16},{20,28},{28,20},{1,9},{9... | collective-permute-start | bytes 9437192 | tf_op jit(solution)/shard_map/ppermute | solution.py:14
  928.3 1.0 copy-start.9
  956.2 0.8 copy-start.16
  1073.4 0.7 copy-start.35
  1075.9 4.3 copy-start.36
  1084.5 1.2 copy-start.23
  1084.5 1.5 copy-start.24
  1093.6 2.0 copy-start.1
  1097.6 136.5 %collective-permute-start.4 = (f32[3,512,512]{1,2,0:T(8,128)}, f32[3,512,512]{1,2,0:T(8,128)}, u32[]{:S(2)}, u32[]{:S(2)}) collective-permute-start(f32[3,512,512]{1,2,0:T(8,128)} %pad_maximum_fusion.16), channel_id=1, source_target_pairs={{0,16},{16,0},{4,20},{20,4},{8,24},{24,8},{12,28},{28,12},{1,17},{... | collective-permute-start | bytes 9437192 | tf_op jit(solution)/shard_map/ppermute | solution.py:14
  1239.7 1.0 copy-start.10
  1267.5 0.8 copy-start.17
  1394.4 7.1 copy-start.5
  1394.5 7.1 copy-start.6
where the time goes:
time: 1410 us; the launch traced here: 1400 us
  other arithmetic  801 us (57%)
  waiting for transfers between devices  339 us (24%)
  matrix products  152 us (11%)
  local copies, waits for them, and re-layouts  99.4 us (7%)
    ppermute x5, waiting for transfers between devices, swapped(): return lax.ppermute(block, axis, route)  339 us
    another operation x72, other arithmetic, blocked_factor(): head_factor = jnp.linalg.cholesky(head)  299 us
    another operation x13, other arithmetic, merge_blocks(): lax.linalg.triangular_solve(factor, coupled, left_side=True, lower=True)  253 us
    another operation x36, other arithmetic, blocked_factor(): lax.linalg.triangular_solve(head_factor, below, left_side=False, lower=Tr...  189 us
    another operation x42, matrix products, merge_blocks(): lax.linalg.triangular_solve(factor, coupled, left_side=True, lower=True)  69.6 us
    another operation x79, local copies, waits for them, and re-layouts, merge_blocks(): lax.linalg.triangular_solve(factor, coupled, left_side=True, lower=True)  69.4 us
    dot_general x6, matrix products, merge_blocks(): lax.dot_general(scaled, scaled, (((0,), (0,)), ((), ())), precision=lax.P...  46.6 us
    add x6, other arithmetic, merge_blocks(): factor = blocked_factor(left_lower + right_upper)  30.2 us
  transfers between devices with their start and end apart: 5, of which 5 were waited for; matrix products, arithmetic and copies ran while one was open for 0% of the time, Pallas kernels for 0%

commit v1 on v0

--- a/solution.py
+++ b/solution.py
@@ -1,7 +1,13 @@
+import functools
 import jax
 import jax.numpy as jnp
 from jax import lax
+from jax.experimental import pallas as pl
+from jax.experimental.pallas import tpu as pltpu
 from jax.sharding import PartitionSpec as P
+
+HIGHEST = lax.Precision.HIGHEST
+AXES = ("slab", "col")
 
 
 def swapped(block, axis, stride):
@@ -130,11 +136,10 @@
     )
 
 
-def local(classes, across_coeff, along_coeff):
+def local_columns(classes, across_coeff, along_coeff):
     across = lookup(classes, across_coeff)
     along = lookup(classes, along_coeff)
-    own_map = strip_map(along[0], across[0])
-    own_map = merge_maps(own_map, strip_map(along[1], across[1]))
+    own_map = piece_map(across, along)
     col_levels = lax.axis_size("col").bit_length() - 1
     slab_levels = lax.axis_size("slab").bit_length() - 1
     merged = own_map
@@ -153,6 +158,262 @@
     return (own_map, root_rows)
 
 
+def sweep_kernel(count, size, x_ref, o_ref):
+    o_ref[...] = x_ref[...]
+    sub = lax.broadcasted_iota(jnp.int32, (1, size, size), 1)
+    lane = lax.broadcasted_iota(jnp.int32, (1, size, size), 2)
+
+    def step(k, carry):
+        group = min(count, 4)
+        for start in range(0, count, group):
+            a = o_ref[start : start + group]
+            row = o_ref[start : start + group, pl.ds(k, 1), :]
+            is_row = sub == k
+            is_col = lane == k
+            col = jnp.sum(jnp.where(is_col, a, 0.0), axis=2, keepdims=True)
+            pivot = jnp.sum(jnp.where(is_col[:, :1], row, 0.0), axis=2, keepdims=True)
+            inv = 1.0 / pivot
+            scaled = row * inv
+            new = a - col * scaled
+            new = jnp.where(is_col, -(col * inv), new)
+            new = jnp.where(is_row, jnp.where(is_col, inv, scaled), new)
+            o_ref[start : start + group] = new
+        return carry
+
+    lax.fori_loop(0, size, step, 0)
+
+
+def inverses(blocks):
+    count, size, _ = blocks.shape
+    return pl.pallas_call(
+        functools.partial(sweep_kernel, count, size),
+        out_shape=jax.ShapeDtypeStruct(blocks.shape, jnp.float32),
+        in_specs=[pl.BlockSpec(memory_space=pltpu.VMEM)],
+        out_specs=pl.BlockSpec(memory_space=pltpu.VMEM),
+    )(blocks)
+
+
+def piece_kernel(size, rows, vec_ref, cols_ref, o_ref, coef):
+    levels = size.bit_length() - 1
+    i = pl.program_id(0)
+
+    def back(x, s):
+        return pltpu.roll(x, s, 1)
+
+    def fore(x, s):
+        return pltpu.roll(x, size - s, 1)
+
+    @pl.when(i == 0)
+    def _():
+        def wide(k):
+            return jnp.broadcast_to(vec_ref[k : k + 1, :], (8, size))
+
+        a0, a1, al0, al1 = wide(0), wide(1), wide(2), wide(3)
+        sh1 = back(al1, 1)
+        diag = a0 + a1 + al1 + sh1
+        inv = 1.0 / diag
+        coef[0] = inv
+        lo = -sh1 * inv
+        hi = -al1 * inv
+        for level in range(levels - 1):
+            s = 1 << level
+            fix = 1.0 / (1.0 - lo * back(hi, s) - hi * fore(lo, s))
+            coef[3 * level + 1] = -lo
+            coef[3 * level + 2] = -hi
+            coef[3 * level + 3] = fix
+            lo, hi = -lo * back(lo, s) * fix, -hi * fore(hi, s) * fix
+        g = lo + hi
+        h = back(g, size // 2)
+        coef[3 * levels - 2] = -g
+        coef[3 * levels - 1] = 1.0 / (1.0 - g * h)
+
+    def co(k):
+        return coef[k, 0:1, :]
+
+    row = lax.broadcasted_iota(jnp.int32, (rows, size), 0) + i * rows
+    col = lax.broadcasted_iota(jnp.int32, (rows, size), 1)
+    x = jnp.where(row == col, co(0), 0.0)
+    for level in range(levels - 1):
+        s = 1 << level
+        x = (x + co(3 * level + 1) * back(x, s) + co(3 * level + 2) * fore(x, s)) * co(3 * level + 3)
+    x = (x + co(3 * levels - 2) * back(x, size // 2)) * co(3 * levels - 1)
+    a0, a1, al0 = vec_ref[0:1, :], vec_ref[1:2, :], vec_ref[2:3, :]
+    sh0 = jnp.broadcast_to(vec_ref[4:5, :], (1, size))
+    r0, r1 = cols_ref[:, 0:1], cols_ref[:, 1:2]
+    vert = jnp.where(row == col, al0 + sh0 + a0, 0.0)
+    vert = vert - jnp.where(row == jnp.where(col == size - 1, 0, col + 1), al0, 0.0)
+    vert = vert - jnp.where(col == jnp.where(row == size - 1, 0, row + 1), sh0, 0.0)
+    x0, x1 = x * a0, x * a1
+    o_ref[0, :, :size] = vert - r0 * x0
+    o_ref[0, :, size:] = -(r0 * x1)
+    o_ref[1, :, :size] = -(r1 * x0)
+    o_ref[1, :, size:] = jnp.where(row == col, a1, 0.0) - r1 * x1
+
+
+def piece_map(across, along):
+    size = across.shape[1]
+    rows = 32
+    vecs = jnp.concatenate([across, along, jnp.roll(along, 1, axis=1), along], axis=0)
+    out = pl.pallas_call(
+        functools.partial(piece_kernel, size, rows),
+        grid=(size // rows,),
+        out_shape=jax.ShapeDtypeStruct((2, size, 2 * size), jnp.float32),
+        in_specs=[
+            pl.BlockSpec((8, size), lambda i: (0, 0)),
+            pl.BlockSpec((rows, 2), lambda i: (i, 0)),
+        ],
+        out_specs=pl.BlockSpec((2, rows, 2 * size), lambda i: (0, i, 0)),
+        scratch_shapes=[pltpu.VMEM((3 * (size.bit_length() - 1), 8, size), jnp.float32)],
+    )(vecs, across.T)
+    return out.reshape(2 * size, 2 * size)
+
+
+def bmm(a, b):
+    return jnp.einsum("bij,bjk->bik", a, b, precision=HIGHEST)
+
+
+def bmm_t(a, b):
+    return jnp.einsum("bji,bjk->bik", a, b, precision=HIGHEST)
+
+
+def t(a):
+    return jnp.swapaxes(a, 1, 2)
+
+
+def row_elements(across, along_prev, along):
+    rows, cols = across.shape
+    spot = lax.broadcasted_iota(jnp.int32, (rows, cols), 1)
+    inner = spot > 0
+    diag = jnp.where(inner, jnp.roll(across, 1, axis=1) + across + along_prev + along, 1.0)
+    off = jnp.where(inner, across, 0.0)
+    i = lax.broadcasted_iota(jnp.int32, (1, cols, cols), 1)
+    j = lax.broadcasted_iota(jnp.int32, (1, cols, cols), 2)
+    bb = jnp.where(i == j, diag[:, :, None], 0.0)
+    bb = bb - jnp.where(j == i + 1, off[:, :, None], 0.0) - jnp.where(i == j + 1, off[:, None, :], 0.0)
+    tb = jnp.where(i == j, -jnp.where(inner, along_prev, 0.0)[:, :, None], 0.0)
+    tt = jnp.zeros_like(bb)
+    first = jnp.where(spot == 1, -across[:, :1], 0.0)
+    last = jnp.where(spot == cols - 1, -across[:, cols - 1 :], 0.0)
+    fb = jnp.stack([first, last], axis=2)
+    return tt, tb, bb, jnp.zeros_like(fb), fb, jnp.zeros((rows, 2, 2), jnp.float32)
+
+
+def merge_elements(parts):
+    (tta, ttb), (tba, tbb), (bba, bbb), (fta, ftb), (fba, fbb), (kka, kkb) = [
+        (p[0::2], p[1::2]) for p in parts
+    ]
+    n, k = tta.shape[1], fta.shape[2]
+    w = jnp.concatenate([t(tba), tbb, fba, ftb], axis=2)
+    z = bmm(inverses(bba + ttb), w)
+    u = bmm_t(w, z)
+    zero = jnp.zeros_like(fta)
+    zk = jnp.zeros_like(kka)
+    kk = jnp.concatenate(
+        [jnp.concatenate([kka, zk], axis=2), jnp.concatenate([zk, kkb], axis=2)], axis=1
+    )
+    return (
+        tta - u[:, :n, :n],
+        -u[:, :n, n : 2 * n],
+        bbb - u[:, n : 2 * n, n : 2 * n],
+        jnp.concatenate([fta, zero], axis=2) - u[:, :n, 2 * n :],
+        jnp.concatenate([zero, fbb], axis=2) - u[:, n : 2 * n, 2 * n :],
+        kk - u[:, 2 * n :, 2 * n :],
+    )
+
+
+def ring_solve(d, link, rhs):
+    count, n = d.shape[0], d.shape[1]
+    if count == 1:
+        return bmm(inverses(d + link + t(link)), rhs)
+    w = jnp.concatenate([t(link[0::2]), link[1::2], rhs[0::2]], axis=2)
+    z = bmm(inverses(d[0::2]), w)
+    u = bmm_t(w[:, :, : 2 * n], z)
+    after = jnp.roll(u, -1, axis=0)
+    d_next = d[1::2] - u[:, n:, n : 2 * n] - after[:, :n, :n]
+    r_next = rhs[1::2] - u[:, n:, 2 * n :] - after[:, :n, 2 * n :]
+    odd = ring_solve(d_next, -u[:, :n, n : 2 * n], r_next)
+    both = jnp.concatenate([jnp.roll(odd, 1, axis=0), odd], axis=1)
+    even = z[:, :, 2 * n :] - bmm(z[:, :, : 2 * n], both)
+    return jnp.stack([even, odd], axis=1).reshape(rhs.shape)
+
+
+def local_rows(classes, across_coeff, along_coeff):
+    own_across = lookup(classes, across_coeff)
+    own_along = lookup(classes, along_coeff)
+    devices = lax.axis_size(AXES)
+    me = lax.axis_index(AXES)
+    size = classes.shape[1]
+    cols = classes.shape[0] * devices
+    height = size // devices
+    everyone = lax.all_gather(classes, AXES, axis=0, tiled=True)
+    own_map = piece_map(own_across, own_along)
+    padded = jnp.concatenate([everyone[:, size - 1 :], everyone], axis=1)
+    mine = lax.dynamic_slice_in_dim(padded, me * height, height + 1, 1)
+    across = lookup(mine, across_coeff).T
+    along = lookup(mine, along_coeff).T
+    parts = row_elements(across[1:], along[:-1], along[1:])
+    while parts[0].shape[0] > 1:
+        parts = merge_elements(parts)
+    tt, tb, bb, ft, fb, kk = [p[0] for p in parts]
+
+    def sides(f):
+        return f.reshape(f.shape[0], height, 2).swapaxes(1, 2).reshape(f.shape[0], 2 * height)
+
+    ft, fb = sides(ft), sides(fb)
+    kk = sides(sides(kk).T)
+    square = jnp.concatenate([tt, tb, bb], axis=0)
+    square, ft, fb, kk = [
+        lax.all_gather(p, AXES, axis=0) for p in (square, ft, fb, kk)
+    ]
+    tt, tb, bb = square[:, :cols], square[:, cols : 2 * cols], square[:, 2 * cols :]
+    share = 2 * size // devices
+    start = me * share
+    side = start // size
+    r0 = start - side * size
+    s0 = r0 // height
+    strip = lax.broadcasted_iota(jnp.int32, (devices, 1, 1), 0)
+
+    def cut(f, a):
+        return lax.dynamic_slice(f, (s0 + a, 0, side * height), (1, f.shape[1], height))[0]
+
+    def at(f, a):
+        return jnp.where(strip == s0 + a, f[None], 0.0)
+
+    def rhs_of(f):
+        return jnp.concatenate([at(cut(f, 0), 0), at(cut(f, 1), 1)], axis=2)
+
+    rhs = rhs_of(fb) + jnp.roll(rhs_of(ft), -1, axis=0)
+    x = ring_solve(bb + jnp.roll(tt, -1, axis=0), tb, rhs)
+    x = jnp.concatenate([jnp.roll(x, 1, axis=0), x], axis=1)
+    f = jnp.concatenate([ft, fb], axis=1)
+    k_rows = jnp.concatenate([at(cut(kk, 0).T, 0), at(cut(kk, 1).T, 1)], axis=1)
+    rows = k_rows - bmm_t(x, f)
+    rows = rows.reshape(devices, share, 2, height).transpose(1, 2, 0, 3).reshape(share, 2 * size)
+
+    first_ac = lookup(everyone[:1], across_coeff)
+    last_ac = lookup(everyone[cols - 1 :], across_coeff)
+    al = lookup(everyone[:1], along_coeff)
+    sh = jnp.roll(al, 1, axis=1)
+    zero = jnp.zeros_like(al)
+    on = jnp.concatenate([first_ac + al + sh, last_ac], axis=1)
+    below = jnp.concatenate([al, zero], axis=1)
+    above = jnp.concatenate([sh, zero], axis=1)
+    row = lax.broadcasted_iota(jnp.int32, (share, 2 * size), 0) + start
+    col = lax.broadcasted_iota(jnp.int32, (share, 2 * size), 1)
+    rows = rows + jnp.where(row == col, on, 0.0)
+    rows = rows - jnp.where((row == (col + 1) % size) & (row < size) & (col < size), below, 0.0)
+    rows = rows - jnp.where((col == (row + 1) % size) & (row < size) & (col < size), above, 0.0)
+    return own_map, rows
+
+
+def local(classes, across_coeff, along_coeff):
+    devices = lax.axis_size(AXES)
+    cols = classes.shape[0] * devices
+    if 4 * cols <= classes.shape[1]:
+        return local_rows(classes, across_coeff, along_coeff)
+    return local_columns(classes, across_coeff, along_coeff)
+
+
 def solution(mesh):
     placed = (P(("slab", "col"), None), P(), P())
     return jax.shard_map(

time: 1410 us -> 376 us (0.27)
  other arithmetic: 801 us -> 13.6 us
  waiting for transfers between devices: 339 us -> 0.02 us
  blocking collectives: 0 us -> 160 us
  Pallas kernels: 0 us -> 136 us
  matrix products: 152 us -> 27.5 us
  local copies, waits for them, and re-layouts: 99.4 us -> 21.5 us
    another operation x131 -> x5, other arithmetic: 754 us -> 0.16 us  [the longest x4 0.15 us: ring_solve(): return jnp.stack([even, odd], axis=1).reshape(rhs.shape)]
    ppermute x5 -> x0, waiting for transfers between devices: 339 us -> none  [swapped(): return lax.ppermute(block, axis, route)]
    all_gather x0 -> x4, blocking collectives: none -> 160 us  [the longest x3 116 us: local_rows(): lax.all_gather(p, AXES, axis=0)]
    pallas_call x0 -> x11, Pallas kernels: none -> 136 us  [the longest x10 122 us: inverses(): pl.pallas_call(functools.partial(sweep_kernel, count, size), out_shape=ja...]
    another operation x60 -> x0, matrix products: 86.7 us -> none  [the longest x42 69.6 us: merge_blocks(): lax.linalg.triangular_solve(factor, coupled, left_side=True, lower=True)]
    another operation x81 -> x9, local copies, waits for them, and re-layouts: 69.4 us -> 0.86 us  [the longest x7 0.78 us: ring_solve(): return jnp.stack([even, odd], axis=1).reshape(rhs.shape)]
    dot_general x24 -> x25, matrix products: 65.4 us -> 27.5 us  [the longest x15 17.3 us: bmm(): return jnp.einsum('bij,bjk->bik', a, b, precision=HIGHEST)]
    add x7 -> x9, other arithmetic: 31.6 us -> 3.44 us  [the longest x3 1.93 us: merge_elements(): z = bmm(inverses(bba + ttb), w)]
  transfers between devices with their start and end apart: 5 -> 1, of which waited for: 5 -> 0; matrix products, arithmetic and copies ran while one was open for 0% -> 2% of each run, Pallas kernels for 0% -> 4%
where the time goes in v1:
time: 376 us; the launch traced here: 374 us
  blocking collectives  160 us (43%)
  Pallas kernels  136 us (36%)
  matrix products  27.5 us (7%)
  local copies, waits for them, and re-layouts  21.5 us (6%)
  between operations  15.2 us (4%)
  other arithmetic  13.6 us (4%)
    pallas_call x10, Pallas kernels, inverses(): pl.pallas_call(functools.partial(sweep_kernel, count, size), out_shape=ja...  122 us
    all_gather x3, blocking collectives, local_rows(): lax.all_gather(p, AXES, axis=0)  116 us
    all_gather x1, blocking collectives, local_rows(): everyone = lax.all_gather(classes, AXES, axis=0, tiled=True)  43.9 us
    dot_general x15, matrix products, bmm(): return jnp.einsum('bij,bjk->bik', a, b, precision=HIGHEST)  17.3 us
    pallas_call x1, Pallas kernels, piece_map(): pl.pallas_call(functools.partial(piece_kernel, size, rows), grid=(size //...  13.7 us
    dot_general x10, matrix products, bmm_t(): return jnp.einsum('bji,bjk->bik', a, b, precision=HIGHEST)  10.2 us
    unnamed x55, local copies, waits for them, and re-layouts  8.69 us
  transfers between devices with their start and end apart: 1, of which 0 were waited for; matrix products, arithmetic and copies ran while one was open for 2% of the time, Pallas kernels for 4%

profile of v1, /device:TPU:0, one launch (start us, length us, event | category | flops | bytes accessed | tf_op | source)
XLA Modules:
  0.0 374.1 jit_solution(8812204190854662959)
XLA Ops:
  7.3 43.9 %all-gather.1 = s32[32,2,512]{2,1,0:T(2,128)S(1)} all-gather(s32[1,2,512]{2,1,0:T(2,128)} %bitcast.214), channel_id=1, replica_groups=mesh['slab'=8,'col'=4] {'slab','col'}, dimensions={0}, use_global_device_ids=true | all-gather | bytes 135168 | tf_op jit(solution)/shard_map/all_gather | solution.py:348
  51.5 0.8 select_reduce_fusion.1
  53.6 0.7 slice.583.x_ref
  54.3 16.8 %shard_map.51 = f32[8,64,64]{2,1,0:T(8,128)} custom-call(f32[8,64,64]{2,1,0:T(8,128)} %slice.583.x_ref), custom_call_target="tpu_custom_call" | custom-call | tf_op jit(solution)/shard_map/pallas_call | solution.py:188
  71.2 1.7 fusion.61
  72.8 1.6 fusion.60
  76.7 9.2 %shard_map.52 = f32[4,64,64]{2,1,0:T(8,128)} custom-call(f32[4,64,64]{2,1,0:T(8,128)} %slice_add_fusion.1.x_ref), custom_call_target="tpu_custom_call" | custom-call | tf_op jit(solution)/shard_map/pallas_call | solution.py:188
  86.0 1.6 fusion.69
  87.6 0.8 fusion.68
  90.1 8.1 %shard_map.53 = f32[2,64,64]{2,1,0:T(8,128)} custom-call(f32[2,64,64]{2,1,0:T(8,128)} %slice_add_fusion.2.x_ref), custom_call_target="tpu_custom_call" | custom-call | tf_op jit(solution)/shard_map/pallas_call | solution.py:188
  98.1 1.2 fusion.82
  101.3 7.6 %shard_map.54 = f32[1,64,64]{2,1,0:T(8,128)} custom-call(f32[1,64,64]{2,1,0:T(8,128)} %slice_add_fusion.3.x_ref), custom_call_target="tpu_custom_call" | custom-call | tf_op jit(solution)/shard_map/pallas_call | solution.py:188
  109.0 1.1 fusion.99
  112.2 38.5 %all_gather.19 = f32[32,32,32]{2,1,0:T(8,128)S(1)} all-gather(f32[1,32,32]{2,1,0:T(8,128)S(1)} %copy.533), channel_id=1, replica_groups=mesh['slab'=8,'col'=4] {'slab','col'}, dimensions={0}, use_global_device_ids=true | all-gather | bytes 135168 | tf_op jit(solution)/shard_map/all_gather | solution.py:366
  151.7 0.9 copy.495
  152.9 39.4 %all_gather.23 = f32[32,64,32]{1,2,0:T(8,128)S(1)} all-gather(f32[1,64,32]{1,2,0:T(8,128)S(1)} %bitcast.196), channel_id=1, replica_groups=mesh['slab'=8,'col'=4] {'slab','col'}, dimensions={0}, use_global_device_ids=true | all-gather | bytes 270336 | tf_op jit(solution)/shard_map/all_gather | solution.py:366
  192.3 38.2 %all_gather.22 = f32[32,64,32]{1,2,0:T(8,128)S(1)} all-gather(f32[1,64,32]{1,2,0:T(8,128)S(1)} %bitcast.195), channel_id=1, replica_groups=mesh['slab'=8,'col'=4] {'slab','col'}, dimensions={0}, use_global_device_ids=true | all-gather | bytes 270336 | tf_op jit(solution)/shard_map/all_gather | solution.py:366
  231.5 0.8 copy-done.6
  232.3 1.0 copy.543
  234.0 13.7 %shard_map.50 = f32[2,512,1024]{2,1,0:T(8,128)} custom-call(f32[8,512]{1,0:T(8,128)} %pad_maximum_fusion.17.vec_ref, f32[512,2]{1,0:T(8,128)} %bitcast.172), custom_call_target="tpu_custom_call" | custom-call | tf_op jit(solution)/shard_map/pallas_call | solution.py:257
  249.4 0.8 broadcast_select_fusion.6
  250.2 0.8 slice.782
  250.9 1.3 slice.781
  252.2 2.0 fusion.149
  254.5 1.0 copy.537.x_ref
  255.5 31.8 %shard_map.55 = f32[16,64,64]{2,1,0:T(8,128)} custom-call(f32[16,64,64]{2,1,0:T(8,128)} %copy.537.x_ref), custom_call_target="tpu_custom_call" | custom-call | tf_op jit(solution)/shard_map/pallas_call | solution.py:188
  287.3 2.4 fusion.5
  289.8 2.8 fusion.20
  292.7 0.9 copy-done.7
  294.2 0.8 copy.544.x_ref
  295.0 16.8 %shard_map.56 = f32[8,64,64]{2,1,0:T(8,128)} custom-call(f32[8,64,64]{2,1,0:T(8,128)} %copy.544.x_ref), custom_call_target="tpu_custom_call" | custom-call | tf_op jit(solution)/shard_map/pallas_call | solution.py:188
  311.8 2.4 fusion.11
  314.1 1.4 fusion.24
  315.7 0.9 copy-done.5
  316.9 0.8 copy.548.x_ref
  317.6 9.2 %shard_map.57 = f32[4,64,64]{2,1,0:T(8,128)} custom-call(f32[4,64,64]{2,1,0:T(8,128)} %copy.548.x_ref), custom_call_target="tpu_custom_call" | custom-call | tf_op jit(solution)/shard_map/pallas_call | solution.py:188
  326.9 1.7 fusion.43
  328.5 0.8 fusion.51
  329.7 0.7 copy.552.x_ref
  330.4 8.1 %shard_map.58 = f32[2,64,64]{2,1,0:T(8,128)} custom-call(f32[2,64,64]{2,1,0:T(8,128)} %copy.552.x_ref), custom_call_target="tpu_custom_call" | custom-call | tf_op jit(solution)/shard_map/pallas_call | solution.py:188
  338.5 1.3 fusion.62
  341.2 7.5 %shard_map.59 = f32[1,64,64]{2,1,0:T(8,128)} custom-call(f32[1,64,64]{2,1,0:T(8,128)} %copy.557.x_ref), custom_call_target="tpu_custom_call" | custom-call | tf_op jit(solution)/shard_map/pallas_call | solution.py:188
  348.8 1.0 fusion.83
  351.0 7.5 %shard_map.60 = f32[1,64,64]{2,1,0:T(8,128)} custom-call(f32[1,64,64]{2,1,0:T(8,128)} %bitcast_add_fusion.1.x_ref), custom_call_target="tpu_custom_call" | custom-call | tf_op jit(solution)/shard_map/pallas_call | solution.py:188
  358.5 1.0 fusion.109
  363.8 1.2 convolution_subtract_fusion
  365.2 1.2 fusion.37
  366.4 0.8 copy.579
  (227 shorter events, 22.5 us)
Async XLA Ops:
  7.2 243.0 %all-gather.5.cloned.1.call-start = ((), (), s32[]{:S(2)}) async-start(), calls=%async_computation | async-start | bytes 2162688 | tf_op jit(solution)/shard_map/all_gather | solution.py:366
  100.3 10.9 %copy-start.9 = (s32[2,512]{1,0:T(2,128)S(1)}, s32[2,512]{1,0:T(2,128)}, u32[]{:S(2)}) copy-start(s32[2,512]{1,0:T(2,128)} %param.3) | copy-start | bytes 12292
  100.3 10.9 %copy-start.10 = (f32[16]{0:T(128)S(1)}, f32[16]{0:T(128)}, u32[]{:S(2)}) copy-start(f32[16]{0:T(128)} %param.4) | copy-start | bytes 196
  100.3 10.9 %copy-start.11 = (f32[16]{0:T(128)S(1)}, f32[16]{0:T(128)}, u32[]{:S(2)}) copy-start(f32[16]{0:T(128)} %param.5) | copy-start | bytes 196
  192.3 38.3 %copy-start = (f32[32,64,32]{1,2,0:T(8,128)}, f32[32,64,32]{1,2,0:T(8,128)S(1)}, u32[]{:S(2)}) copy-start(f32[32,64,32]{1,2,0:T(8,128)S(1)} %all_gather.23) | copy-start | bytes 786436
  230.5 0.8 copy-start.2
  231.5 0.8 copy-start.6
  292.5 1.0 copy-start.7
  294.0 1.1 copy-start.4
  315.5 1.0 copy-start.5
  362.5 1.0 copy-start.1
  362.5 1.2 copy-start.3
  362.5 1.2 copy-start.8
Sparse Core Ops, SparseCore 0:
  111.3 53.3 all-gather.4
